TPU v7x, 256 devices: a whole 4x4x8 slice. The times are simulated.
256 devices in a mesh: seq: 32 (over y_hi, z, core), head: 8 (over y_lo, x).
Axes of the slice: x: 4, y: 4 (y_hi: 2, y_lo: 2; y = y_hi * 2 + y_lo), z: 8, core: 2. Of those that a mesh axis runs over, the one named last changes fastest.
Arguments:
- q_cells: bfloat16 [8192, 8192], P('seq', 'head'), may hold values from -60 to 60
- k_cells: bfloat16 [8192, 1024], P('seq', 'head'), may hold values from -11 to 11
- v_cells: bfloat16 [8192, 1024], P('seq', 'head'), may hold values from -6 to 6
- do_cells: bfloat16 [8192, 8192], P('seq', 'head'), may hold values from -6 to 6
- q_head: bfloat16 [1024, 8192], P('seq', 'head'), may hold values from -60 to 60
- k_head: bfloat16 [1024, 1024], P('seq', 'head'), may hold values from -6 to 6
- v_head: bfloat16 [1024, 1024], P('seq', 'head'), may hold values from -6 to 6
- do_head: bfloat16 [1024, 8192], P('seq', 'head'), may hold values from -6 to 6
- vis_mask: int32 [64, 8], P('seq'), may hold values from 0 to 1, as said below
Outputs:
- dq_cells: bfloat16 [8192, 8192], P('seq', 'head')
- dk_cells: bfloat16 [8192, 1024], P('seq', 'head')
- dv_cells: bfloat16 [8192, 1024], P('seq', 'head')
- dq_head: bfloat16 [1024, 8192], P('seq', 'head')
- dk_head: bfloat16 [1024, 1024], P('seq', 'head')
- dv_head: bfloat16 [1024, 1024], P('seq', 'head')
Inputs may be any that keep to these rules, and one draw needn't show every extreme that they name: vis_mask[b, t] = 1 lets the cells of block b see the headers of block t.
All inputs are finite; a program needn't handle non-finite values.
Results may differ from a plain program's by a relative error of at most 0.012.
Values may be sent and summed in bfloat16 or wider, within the bound.
A program may use at most 64 MiB of HBM per device.

v0:
```python
from functools import partial
import jax
import jax.numpy as jnp
from jax import lax
from jax.sharding import PartitionSpec as P

HD = 128
W = 256
BLOCK = 128
masked_score = -1e30


def product(pattern, former, latter):
    return jnp.einsum(pattern, former, latter, preferred_element_type=jnp.float32)


def block_stats(queries, key_rows, visible, scaling):
    scores = product("nkgd,mkd->kgnm", queries, key_rows) * scaling
    kept_scores = jnp.where(visible, scores, masked_score)
    highest = jnp.max(kept_scores, axis=-1)
    totals = jnp.sum(jnp.where(visible, jnp.exp(scores - highest[..., None]), 0.0), axis=-1)
    return (highest, totals)


def merge_stats(former, latter):
    highest = jnp.maximum(former[0], latter[0])
    return (
        highest,
        former[1] * jnp.exp(former[0] - highest) + latter[1] * jnp.exp(latter[0] - highest),
    )


def weights_of(queries, key_rows, log_totals, visible, scaling):
    scores = product("nkgd,mkd->kgnm", queries, key_rows) * scaling
    return jnp.where(visible, jnp.exp(scores - log_totals[..., None]), 0.0)


def block_delta(queries, grads_out, key_rows, value_rows, log_totals, visible, scaling):
    weights = weights_of(queries, key_rows, log_totals, visible, scaling)
    slopes = product("nkgd,mkd->kgnm", grads_out, value_rows)
    return jnp.sum(weights * slopes, axis=-1)


def block_grads(queries, grads_out, key_rows, value_rows, log_totals, deltas, visible, scaling):
    weights = weights_of(queries, key_rows, log_totals, visible, scaling)
    slopes = product("nkgd,mkd->kgnm", grads_out, value_rows)
    score_grads = weights * (slopes - deltas[..., None])
    weight_low = weights.astype(jnp.bfloat16)
    grad_low = score_grads.astype(jnp.bfloat16)
    grad_values = product("kgnm,nkgd->mkd", weight_low, grads_out)
    grad_keys = product("kgnm,nkgd->mkd", grad_low, queries) * scaling
    grad_queries = product("kgnm,mkd->nkgd", grad_low, key_rows) * scaling
    return (grad_queries, grad_keys, grad_values)


def to_rows(values):
    return jnp.transpose(values, (1, 2, 0, 3)).reshape(values.shape[1], values.shape[2], -1)


def from_rows(values, pieces):
    return jnp.transpose(values.reshape(values.shape[0], values.shape[1], pieces, -1), (2, 0, 1, 3))


def guarded(function, operands):
    return function(*operands)


def per_device(q_cells, k_cells, v_cells, do_cells, q_head, k_head, v_head, do_head, vis_mask):
    cell_count = q_cells.shape[0]
    kv_local = k_cells.shape[1] // HD
    query_local = q_cells.shape[1] // HD
    groups = query_local // kv_local
    scaling = HD ** (-0.5)
    regions = cell_count // W
    own_rows = q_head.shape[0]
    head_keys, head_values = (
        lax.all_gather(k_head, "seq", axis=0, tiled=True),
        lax.all_gather(v_head, "seq", axis=0, tiled=True),
    )
    all_queries, all_grads = (
        lax.all_gather(q_head, "seq", axis=0, tiled=True),
        lax.all_gather(do_head, "seq", axis=0, tiled=True),
    )
    header_count = head_keys.shape[0]
    blocks = header_count // BLOCK
    cell_query = q_cells.reshape(cell_count, kv_local, groups, HD)
    cell_grad = do_cells.reshape(cell_count, kv_local, groups, HD)
    cell_key = k_cells.reshape(cell_count, kv_local, HD)
    cell_value = v_cells.reshape(cell_count, kv_local, HD)
    region_query = q_cells.reshape(regions, W, kv_local, groups, HD)
    region_grad = do_cells.reshape(regions, W, kv_local, groups, HD)
    region_key = k_cells.reshape(regions, W, kv_local, HD)
    region_value = v_cells.reshape(regions, W, kv_local, HD)
    header_key_rows = head_keys.reshape(header_count, kv_local, HD)
    header_value_rows = head_values.reshape(header_count, kv_local, HD)
    key_blocks = head_keys.reshape(blocks, BLOCK, kv_local, HD)
    value_blocks = head_values.reshape(blocks, BLOCK, kv_local, HD)
    seen_blocks = jnp.transpose(jnp.repeat(vis_mask, BLOCK, axis=0) > 0)

    def outer_stat(operands):
        key_block, seen_column = operands
        return guarded(
            partial(block_stats, cell_query, scaling=scaling), (key_block, seen_column[:, None])
        )

    block_highest, block_totals = lax.map(outer_stat, (key_blocks, seen_blocks))
    outer_highest = jnp.max(block_highest, axis=0)
    outer_totals = jnp.sum(block_totals * jnp.exp(block_highest - outer_highest), axis=0)
    local_stats = jax.vmap(partial(block_stats, visible=True, scaling=scaling))(
        region_query, region_key
    )
    highest, totals = merge_stats(
        (to_rows(local_stats[0]), to_rows(local_stats[1])), (outer_highest, outer_totals)
    )
    cell_log = highest + jnp.log(totals)
    region_log = from_rows(cell_log, regions)

    def outer_delta(operands):
        key_block, value_block, seen_column = operands
        return guarded(
            partial(block_delta, cell_query, cell_grad, scaling=scaling),
            (key_block, value_block, cell_log, seen_column[:, None]),
        )

    local_delta = to_rows(
        jax.vmap(partial(block_delta, visible=True, scaling=scaling))(
            region_query, region_grad, region_key, region_value, region_log
        )
    )
    cell_delta = local_delta + jnp.sum(
        lax.map(outer_delta, (key_blocks, value_blocks, seen_blocks)), axis=0
    )
    query_zeros = jnp.zeros((cell_count, kv_local, groups, HD), jnp.float32)

    def outer_grad(running, operands):
        key_block, value_block, seen_column = operands
        gradients = guarded(
            partial(block_grads, cell_query, cell_grad, scaling=scaling),
            (key_block, value_block, cell_log, cell_delta, seen_column[:, None]),
        )
        return (running + gradients[0], (gradients[1], gradients[2]))

    outer_query, (key_parts, value_parts) = lax.scan(
        outer_grad, query_zeros, (key_blocks, value_blocks, seen_blocks)
    )
    local_grads = jax.vmap(partial(block_grads, visible=True, scaling=scaling))(
        region_query,
        region_grad,
        region_key,
        region_value,
        region_log,
        from_rows(cell_delta, regions),
    )
    query_blocks = all_queries.reshape(blocks, BLOCK, kv_local, groups, HD)
    grad_blocks = all_grads.reshape(blocks, BLOCK, kv_local, groups, HD)
    own_query = q_head.reshape(own_rows, kv_local, groups, HD)
    own_grad = do_head.reshape(own_rows, kv_local, groups, HD)
    first_row = lax.axis_index("seq") * own_rows

    def own_slice(values):
        return lax.dynamic_slice_in_dim(values, first_row, own_rows, 2)

    def own_update(values, replaced):
        return lax.dynamic_update_slice_in_dim(values, replaced, first_row, 2)

    cross_stats = lax.map(
        lambda operands: block_stats(operands, cell_key, True, scaling), query_blocks
    )
    cross_highest = to_rows(cross_stats[0])
    cross_totals = to_rows(cross_stats[1])
    self_stats = block_stats(own_query, header_key_rows, True, scaling)
    own_merged = merge_stats((own_slice(cross_highest), own_slice(cross_totals)), self_stats)
    part_highest = own_update(cross_highest, own_merged[0])
    part_totals = own_update(cross_totals, own_merged[1])
    head_highest = lax.pmax(part_highest.astype(jnp.bfloat16), "seq").astype(part_highest.dtype)
    head_totals = lax.psum(part_totals * jnp.exp(part_highest - head_highest), "seq")
    head_log = head_highest + jnp.log(head_totals)
    block_log = from_rows(head_log, blocks)
    own_log = own_slice(head_log)
    cross_delta = to_rows(
        lax.map(
            lambda operands: block_delta(
                operands[0], operands[1], cell_key, cell_value, operands[2], True, scaling
            ),
            (query_blocks, grad_blocks, block_log),
        )
    )
    self_delta = block_delta(
        own_query, own_grad, header_key_rows, header_value_rows, own_log, True, scaling
    )
    part_delta = own_update(cross_delta, own_slice(cross_delta) + self_delta)
    head_delta = lax.psum(part_delta, "seq")
    block_deltas = from_rows(head_delta, blocks)
    own_delta = own_slice(head_delta)
    key_zeros = jnp.zeros((cell_count, kv_local, HD), jnp.float32)

    def cross_grad(running, operands):
        gradients = block_grads(
            operands[0], operands[1], cell_key, cell_value, operands[2], operands[3], True, scaling
        )
        return ((running[0] + gradients[1], running[1] + gradients[2]), gradients[0])

    (cross_key, cross_value), cross_query = lax.scan(
        cross_grad, (key_zeros, key_zeros), (query_blocks, grad_blocks, block_log, block_deltas)
    )
    self_grads = block_grads(
        own_query, own_grad, header_key_rows, header_value_rows, own_log, own_delta, True, scaling
    )
    query_part = cross_query.reshape(header_count, query_local * HD)
    key_part = key_parts.reshape(header_count, kv_local * HD) + self_grads[1].reshape(
        header_count, kv_local * HD
    )
    value_part = value_parts.reshape(header_count, kv_local * HD) + self_grads[2].reshape(
        header_count, kv_local * HD
    )
    whole_sums = lax.psum((query_part, key_part, value_part), "seq")
    query_sum, key_sum, value_sum = [
        lax.dynamic_slice_in_dim(summed, first_row, own_rows, 0) for summed in whole_sums
    ]
    dq_cells = (
        local_grads[0].reshape(cell_count, query_local * HD)
        + outer_query.reshape(cell_count, query_local * HD)
    ).astype(jnp.bfloat16)
    dk_cells = (
        local_grads[1].reshape(cell_count, kv_local * HD)
        + cross_key.reshape(cell_count, kv_local * HD)
    ).astype(jnp.bfloat16)
    dv_cells = (
        local_grads[2].reshape(cell_count, kv_local * HD)
        + cross_value.reshape(cell_count, kv_local * HD)
    ).astype(jnp.bfloat16)
    dq_head = (query_sum + self_grads[0].reshape(own_rows, query_local * HD)).astype(jnp.bfloat16)
    return (
        dq_cells,
        dk_cells,
        dv_cells,
        dq_head,
        key_sum.astype(jnp.bfloat16),
        value_sum.astype(jnp.bfloat16),
    )


def solution(mesh):
    return jax.shard_map(
        per_device,
        mesh=mesh,
        in_specs=(
            P("seq", "head"),
            P("seq", "head"),
            P("seq", "head"),
            P("seq", "head"),
            P("seq", "head"),
            P("seq", "head"),
            P("seq", "head"),
            P("seq", "head"),
            P("seq", None),
        ),
        out_specs=(
            P("seq", "head"),
            P("seq", "head"),
            P("seq", "head"),
            P("seq", "head"),
            P("seq", "head"),
            P("seq", "head"),
        ),
        check_vma=False,
    )
```

profile of v0, /device:TPU:1, one launch (start us, length us, event | category | flops | bytes accessed | tf_op | source)
XLA Modules:
  0.0 988.0 jit_solution(11837171689813258582)
XLA Ops:
  9.5 47.2 %all_gather.12 = bf16[1024,128]{1,0:T(8,128)(2,1)S(1)} all-gather(bf16[32,128]{1,0:T(8,128)(2,1)} %param.26), channel_id=1, replica_groups=mesh['seq'=32,'head'=8] {'seq'}, dimensions={0}, use_global_device_ids=true | all-gather | bytes 270336 | tf_op jit(solution)/shard_map/all_gather | solution.py:77
  56.7 40.4 %all_gather.13 = bf16[1024,128]{1,0:T(8,128)(2,1)} all-gather(bf16[32,128]{1,0:T(8,128)(2,1)} %param.27), channel_id=1, replica_groups=mesh['seq'=32,'head'=8] {'seq'}, dimensions={0}, use_global_device_ids=true | all-gather | bytes 270336 | tf_op jit(solution)/shard_map/all_gather | solution.py:78
  98.7 4.6 while.74
  104.2 1.5 bitcast_reduce_fusion
  109.0 16.5 %while.75 = (s32[]{:T(128)}, f32[8,1,8,256]{3,2,1,0:T(8,128)}, pred[8,256]{1,0:T(8,128)(4,1)S(1)}, bf16[8,128,1,128]{3,1,2,0:T(8,128)(2,1)S(1)}, bf16[256,1,8,12...) while((s32[]{:T(128)}, f32[8,1,8,256]{3,2,1,0:T(8,128)}, ...), condition=%wide.region_11.12_spmd, body=%wide.region_9.11_spmd.sunk | while | flops 135526400 | bytes 3245173 | solution.py:131
  125.5 1.4 reduce_sum.103
  127.8 3.0 fusion.95
  133.0 2.2 copy.97
  135.3 1.9 copy.67
  137.2 37.2 %all-gather.5.cloned.1.call-done = bf16[1024,1024]{1,0:T(8,128)(2,1)} async-done(((bf16[32,1024]{1,0:T(8,128)(2,1)}), bf16[1024,1024]{1,0:T(8,128)(2,1)}) %all-gather.5.cloned.1.call-update) | async-done | bytes 2097168 | tf_op jit(solution)/shard_map/all_gather | solution.py:82
  174.4 2.2 copy.98
  176.6 1.9 copy.68
  179.8 18.8 %while.76 = (s32[]{:T(128)}, f32[8,1,8,128]{3,2,1,0:T(8,128)}, f32[8,1,8,128]{3,2,1,0:T(8,128)}, bf16[8,128,1,8,128]{4,1,3,2,0:T(8,128)(2,1)}, bf16[256,1,128]{2,0,1:T(8,128)(2,1)S(1)}, /*index=5*/s32[]{:T(128)}) while((s32[]{:T(128)}, f32[8,1,8,128]{3,2,1,0:T(8,128)}, f32[8,1,8,128]{3,2,1,0:T(8,128)}, ...), condition=%wide.region_18.19_spmd, body=%wide.region_15.18_spmd.sunk | while | flops 68155392 | bytes 2453589 | solution.py:166
  179.8 1.4 fusion.227
  182.1 1.3 fusion.227
  184.5 1.3 fusion.227
  186.8 1.4 fusion.227
  189.1 1.3 fusion.227
  191.5 1.3 fusion.227
  193.8 1.3 fusion.227
  196.2 1.4 fusion.227
  198.5 1.4 fusion.157
  199.9 1.5 dynamic_update_slice.41
  201.4 1.5 dynamic_update_slice.40
  202.8 1.4 convert_element_type.50
  204.2 124.3 %pmax.7 = bf16[1,8,1024]{2,1,0:T(8,128)(2,1)} all-reduce(bf16[1,8,1024]{2,1,0:T(8,128)(2,1)} %convert_element_type.50), channel_id=1, replica_groups=mesh['seq'=32,'head'=8] {'seq'}, use_global_device_ids=true, to_apply=%region_20.21 | all-reduce | flops 8192 | bytes 32768 | tf_op jit(solution)/shard_map/pmax | solution.py:175
  328.5 1.4 fusion.148
  329.9 128.5 %psum.35 = f32[1,8,1024]{2,1,0:T(8,128)} all-reduce(f32[1,8,1024]{2,1,0:T(8,128)} %fusion.148), channel_id=1, replica_groups=mesh['seq'=32,'head'=8] {'seq'}, use_global_device_ids=true, to_apply=%region_22.23 | all-reduce | flops 8192 | bytes 65536 | tf_op jit(solution)/shard_map/psum | solution.py:176
  460.5 31.5 %while.77 = (s32[]{:T(128)}, f32[8,1,8,128]{3,2,1,0:T(8,128)}, bf16[8,128,1,8,128]{4,1,3,2,0:T(8,128)(2,1)}, bf16[256,1,128]{2,0,1:T(8,128)(2,1)S(1)}, f32[8,1,8...) while((s32[]{:T(128)}, f32[8,1,8,128]{3,2,1,0:T(8,128)}, ...), condition=%wide.region_25.26_spmd, body=%wide.region_23.25_spmd.sunk | while | flops 135265280 | bytes 2777197 | solution.py:181
  462.4 1.4 fusion.233
  466.4 1.4 fusion.233
  470.3 1.4 fusion.233
  474.2 1.4 fusion.233
  478.2 1.4 fusion.233
  482.1 1.4 fusion.233
  486.0 1.4 fusion.233
  490.0 1.4 fusion.233
  491.9 2.6 multiply_reduce_fusion
  494.5 1.4 bitcast_add_fusion.1
  495.9 1.5 dynamic_update_slice.42
  497.3 128.5 %psum.36 = f32[1,8,1024]{2,1,0:T(8,128)} all-reduce(f32[1,8,1024]{2,1,0:T(8,128)} %dynamic_update_slice.42), channel_id=1, replica_groups=mesh['seq'=32,'head'=8] {'seq'}, use_global_device_ids=true, to_apply=%region_27.28 | all-reduce | flops 8192 | bytes 65536 | tf_op jit(solution)/shard_map/psum | solution.py:192
  625.9 63.3 %while.79 = (s32[]{:T(128)}, f32[256,1,128]{0,2,1:T(8,128)}, f32[256,1,128]{0,2,1:T(8,128)}, f32[8,128,1,8,128]{4,3,1,0,2:T(8,128)}, bf16[8,128,1,8,128]{4,1,3,2...) while((s32[]{:T(128)}, f32[256,1,128]{0,2,1:T(8,128)}, ...), condition=%wide.region_29.30_spmd.clone, body=%wide.region_28.29_spmd.clone.sunk | while | flops 337412096 | bytes 9134296 | solution.py:203
  627.9 1.9 fusion.262
  635.8 1.9 fusion.262
  642.4 1.3 fusion.259
  643.7 1.9 fusion.262
  650.3 1.3 fusion.259
  651.6 1.9 fusion.262
  658.2 1.3 fusion.259
  659.5 1.9 fusion.262
  667.4 1.9 fusion.262
  675.4 1.9 fusion.262
  683.3 1.9 fusion.262
  689.2 5.1 copy.144
  694.9 39.1 %while.78 = (s32[]{:T(128)}, f32[256,1,8,128]{0,3,2,1:T(8,128)}, f32[8,128,1,128]{3,1,2,0:T(8,128)}, f32[8,128,1,128]{3,1,2,0:T(8,128)}, bf16[8,128,1,128]{3,1,2...) while((s32[]{:T(128)}, f32[256,1,8,128]{0,3,2,1:T(8,128)}, ...), condition=%wide.region_14.15_spmd.clone, body=%wide.region_13.14_spmd.clone.sunk | while | flops 338182144 | bytes 17548512 | solution.py:143
  734.1 2.5 copy.83
  736.6 2.1 fusion.114
  738.7 1.4 convolution_multiply_fusion.8
  740.1 2.5 copy.60
  742.7 2.6 add_convert_fusion
  749.5 140.0 %all-reduce.5 = (bf16[1024,128]{1,0:T(8,128)(2,1)S(1)}, bf16[1024,128]{1,0:T(8,128)(2,1)}) all-reduce(f32[1024,128]{1,0:T(8,128)} %fusion.104, f32[1024,128]{1,0:T(8,128)} %fusion.105), channel_id=1, replica_groups=mesh['seq'=32,'head'=8] {'seq'}, use_global_device_ids=true, to_apply=%region_31.32 | all-reduce | flops 262144 | bytes 1572864 | tf_op jit(solution)/shard_map/psum | solution.py:216
  890.8 2.4 fusion.111
  894.4 85.6 %all-reduce.4.cloned.1.call-done = f32[1024,1024]{1,0:T(8,128)} async-done(((f32[1024,1024]{1,0:T(8,128)}), f32[1024,1024]{1,0:T(8,128)}) %all-reduce.4.cloned.1.call-update) | async-done | bytes 4194320 | tf_op jit(solution)/shard_map/psum | solution.py:216
  979.9 1.6 fusion.135
  (362 shorter events, 153.0 us)
Async XLA Ops:
  7.2 125.9 %all-gather.3.cloned.1.call-start = ((), (), s32[]{:S(2)}) async-start(), calls=%async_computation | async-start | bytes 2162688 | tf_op jit(solution)/shard_map/all_gather | solution.py:81
  7.9 166.5 %all-gather.5.cloned.1.call-start = ((), (), s32[]{:S(2)}) async-start(), calls=%async_computation.1 | async-start | bytes 2162688 | tf_op jit(solution)/shard_map/all_gather | solution.py:82
  8.6 971.3 %all-reduce.4.cloned.1.call-start = ((), (), s32[]{:S(2)}) async-start(), calls=%async_computation.2 | async-start | bytes 8388608 | tf_op jit(solution)/shard_map/psum | solution.py:216
  98.7 4.6 copy-start.9
  103.3 0.6 copy-start.15
  103.3 0.9 copy-start.2
  105.7 1.5 copy-start.23
  106.4 1.3 copy-start.24
  107.2 1.8 copy-start.26
  107.6 1.4 copy-start.25
  109.0 18.7 %copy-start.5 = (bf16[256,128]{1,0:T(8,128)(2,1)S(1)}, bf16[256,128]{1,0:T(8,128)(2,1)}, u32[]{:S(2)}) copy-start(bf16[256,128]{1,0:T(8,128)(2,1)} %param.23) | copy-start | bytes 196612
  125.5 5.2 copy-start.19
  127.8 3.0 copy-start.21
  127.8 3.0 copy-start.29
  127.8 3.0 copy-start.16
  131.2 1.0 copy-start.3
  131.2 1.0 copy-start.27
  459.2 1.3 copy-start.18
  626.6 4.5 copy-start.6
  632.3 1.4 copy-start.7
  634.5 4.5 copy-start.6
  640.2 1.4 copy-start.7
  642.4 4.5 copy-start.6
  648.2 1.4 copy-start.7
  650.3 4.5 copy-start.6
  656.1 1.4 copy-start.7
  658.2 4.5 copy-start.6
  664.0 1.4 copy-start.7
  666.1 4.5 copy-start.6
  671.9 1.4 copy-start.7
  674.1 4.5 copy-start.6
  679.8 1.4 copy-start.7
  682.0 4.5 copy-start.6
  687.7 1.4 copy-start.7
  694.3 0.7 copy-start.20
  695.3 3.0 copy-start
  698.8 1.1 copy-start.1
  700.2 3.0 copy-start
  703.7 1.1 copy-start.1
  705.1 3.0 copy-start
  708.6 1.1 copy-start.1
  710.0 3.0 copy-start
  713.5 1.1 copy-start.1
  714.9 3.0 copy-start
  718.3 1.1 copy-start.1
  719.8 3.0 copy-start
  723.2 1.1 copy-start.1
  724.7 3.0 copy-start
  728.1 1.1 copy-start.1
  729.6 3.0 copy-start
  733.0 1.1 copy-start.1
  734.1 2.5 copy-start.22
  738.7 1.4 copy-start.12
  740.1 6.0 copy-start.28
  742.7 3.5 copy-start.4
  742.7 3.5 copy-start.13
  745.3 1.5 copy-start.17
  745.3 1.5 copy-start.31
  746.4 1.6 copy-start.14
  746.5 1.6 copy-start.30
  746.9 2.4 copy-start.8
  746.9 2.5 copy-start.11
  749.3 143.9 %copy-start.10 = (bf16[256,1024]{1,0:T(8,128)(2,1)S(1)}, bf16[256,1024]{1,0:T(8,128)(2,1)}, u32[]{:S(2)}) copy-start(bf16[256,1024]{1,0:T(8,128)(2,1)} %param.24) | copy-start | bytes 1572868
Sparse Core Ops, SparseCore 0:
  10.8 84.3 all-gather.2
  98.0 76.3 all-gather.4
  694.4 285.4 all-reduce.3
where the time goes:
time: 992 us; the launch traced here: 988 us
  blocking collectives  609 us (61%)
  matrix products  139 us (14%)
  waiting for transfers between devices  124 us (12%)
  local copies, waits for them, and re-layouts  76.3 us (8%)
  other arithmetic  23.8 us (2%)
  between operations  14.2 us (1%)
    psum x1, blocking collectives, per_device(): whole_sums = lax.psum((query_part, key_part, value_part), 'seq')  140 us
    dot_general x138, matrix products, product(): jnp.einsum(pattern, former, latter, preferred_element_type=jnp.float32)  139 us
    psum x1, blocking collectives, per_device(): head_delta = lax.psum(part_delta, 'seq')  129 us
    psum x1, blocking collectives, per_device(): lax.psum(part_totals * jnp.exp(part_highest - head_highest), 'seq')  128 us
    pmax x1, blocking collectives, per_device(): lax.pmax(part_highest.astype(jnp.bfloat16), 'seq')  124 us
    psum x1, waiting for transfers between devices, per_device(): whole_sums = lax.psum((query_part, key_part, value_part), 'seq')  85.6 us
    all_gather x1, blocking collectives, per_device(): lax.all_gather(k_head, 'seq', axis=0, tiled=True)  47.2 us
    all_gather x1, blocking collectives, per_device(): lax.all_gather(v_head, 'seq', axis=0, tiled=True)  40.4 us
  transfers between devices with their start and end apart: 3, of which 2 were waited for; matrix products, arithmetic and copies ran while one was open for 9% of the time, Pallas kernels for 0%

commit v1 on v0

--- a/solution.py
+++ b/solution.py
@@ -1,3 +1,4 @@
+import functools
 from functools import partial
 import jax
 import jax.numpy as jnp
@@ -8,6 +9,16 @@
 W = 256
 BLOCK = 128
 masked_score = -1e30
+
+
+def units_lead(incoming_x, which_axis):
+    response = lax.all_to_all(
+        jnp.stack([incoming_x for _ in range(lax.axis_size(which_axis))]), which_axis, 0, 0
+    )
+    return jnp.concatenate(response, axis=0)
+
+
+fill_the_numbers = functools.partial(units_lead, which_axis="seq")
 
 
 def product(pattern, former, latter):
@@ -75,7 +86,7 @@
     own_rows = q_head.shape[0]
     head_keys, head_values = (
         lax.all_gather(k_head, "seq", axis=0, tiled=True),
-        lax.all_gather(v_head, "seq", axis=0, tiled=True),
+        fill_the_numbers(v_head),
     )
     all_queries, all_grads = (
         lax.all_gather(q_head, "seq", axis=0, tiled=True),

time: 992 us -> 992 us (level)
  blocking collectives: 609 us -> 564 us
  waiting for transfers between devices: 124 us -> 147 us
  starting transfers between devices: 0.11 us -> 12.9 us
    all_gather x1 -> x0, blocking collectives: 40.4 us -> none  [per_device(): lax.all_gather(v_head, 'seq', axis=0, tiled=True)]
    all_gather x1, waiting for transfers between devices: 37.2 us -> 59.9 us  [per_device(): lax.all_gather(do_head, 'seq', axis=0, tiled=True)]
    all_to_all x0 -> x1, starting transfers between devices: none -> 12.8 us  [units_lead(): lax.all_to_all(jnp.stack([incoming_x for _ in range(lax.axis_size(which_a...]
  transfers between devices with their start and end apart: 3 -> 4, of which waited for: 2 -> 2; matrix products, arithmetic and copies ran while one was open for 9% -> 10% of each run, Pallas kernels for 0% -> 0%
where the time goes in v1:
time: 992 us; the launch traced here: 988 us
  blocking collectives  564 us (57%)
  waiting for transfers between devices  147 us (15%)
  matrix products  140 us (14%)
  local copies, waits for them, and re-layouts  83.5 us (8%)
  other arithmetic  25.6 us (3%)
  between operations  14 us (1%)
  starting transfers between devices  12.9 us (1%)
    psum x1, blocking collectives, per_device(): whole_sums = lax.psum((query_part, key_part, value_part), 'seq')  140 us
    dot_general x138, matrix products, product(): jnp.einsum(pattern, former, latter, preferred_element_type=jnp.float32)  140 us
    psum x1, blocking collectives, per_device(): head_delta = lax.psum(part_delta, 'seq')  129 us
    psum x1, blocking collectives, per_device(): lax.psum(part_totals * jnp.exp(part_highest - head_highest), 'seq')  128 us
    pmax x1, blocking collectives, per_device(): lax.pmax(part_highest.astype(jnp.bfloat16), 'seq')  124 us
    psum x1, waiting for transfers between devices, per_device(): whole_sums = lax.psum((query_part, key_part, value_part), 'seq')  85.3 us
    all_gather x1, waiting for transfers between devices, per_device(): lax.all_gather(do_head, 'seq', axis=0, tiled=True)  59.9 us
    all_gather x1, blocking collectives, per_device(): lax.all_gather(k_head, 'seq', axis=0, tiled=True)  42.9 us
  transfers between devices with their start and end apart: 4, of which 2 were waited for; matrix products, arithmetic and copies ran while one was open for 10% of the time, Pallas kernels for 0%

profile of v1, /device:TPU:1, one launch (start us, length us, event | category | flops | bytes accessed | tf_op | source)
XLA Modules:
  0.0 987.9 jit_solution(4535811208277397065)
XLA Ops:
  7.9 1.4 stack.2
  9.3 12.8 %all-to-all-start = ((bf16[32,32,128]{2,1,0:T(8,128)(2,1)}), bf16[32,32,128]{2,1,0:T(8,128)(2,1)}, u32[]{:S(2)}, u32[]{:S(2)}) async-start(bf16[32,32,128]{2,1,0:T(8,128)(2,1)} %stack.2), calls=%async_computation | async-start | bytes 524288 | tf_op jit(solution)/shard_map/all_to_all | solution.py:15
  23.7 42.9 %all_gather.9 = bf16[1024,128]{1,0:T(8,128)(2,1)S(1)} all-gather(bf16[32,128]{1,0:T(8,128)(2,1)} %param.26), channel_id=1, replica_groups=mesh['seq'=32,'head'=8] {'seq'}, dimensions={0}, use_global_device_ids=true | all-gather | bytes 270336 | tf_op jit(solution)/shard_map/all_gather | solution.py:88
  68.7 9.2 while.74
  85.3 2.1 exponential_reduce_fusion.1
  87.4 3.5 fusion.95
  91.6 16.5 %while.75 = (s32[]{:T(128)}, f32[8,1,8,256]{3,2,1,0:T(8,128)}, pred[8,256]{1,0:T(8,128)(4,1)S(1)}, bf16[8,128,1,128]{3,1,2,0:T(8,128)(2,1)S(1)}, bf16[256,1,8,12...) while((s32[]{:T(128)}, f32[8,1,8,256]{3,2,1,0:T(8,128)}, ...), condition=%wide.region_11.12_spmd, body=%wide.region_9.11_spmd.sunk | while | flops 135526400 | bytes 3245173 | solution.py:142
  108.1 1.4 reduce_sum.103
  110.3 2.2 copy.93
  112.5 1.9 copy.63
  114.5 59.9 %all-gather.5.cloned.1.call-done = bf16[1024,1024]{1,0:T(8,128)(2,1)} async-done(((bf16[32,1024]{1,0:T(8,128)(2,1)}), bf16[1024,1024]{1,0:T(8,128)(2,1)}) %all-gather.5.cloned.1.call-update) | async-done | bytes 2097168 | tf_op jit(solution)/shard_map/all_gather | solution.py:93
  174.4 2.2 copy.94
  176.6 1.9 copy.64
  179.7 18.8 %while.76 = (s32[]{:T(128)}, f32[8,1,8,128]{3,2,1,0:T(8,128)}, f32[8,1,8,128]{3,2,1,0:T(8,128)}, bf16[8,128,1,8,128]{4,1,3,2,0:T(8,128)(2,1)}, bf16[256,1,128]{2,0,1:T(8,128)(2,1)S(1)}, /*index=5*/s32[]{:T(128)}) while((s32[]{:T(128)}, f32[8,1,8,128]{3,2,1,0:T(8,128)}, f32[8,1,8,128]{3,2,1,0:T(8,128)}, ...), condition=%wide.region_18.19_spmd, body=%wide.region_15.18_spmd.sunk | while | flops 68155392 | bytes 2453589 | solution.py:177
  179.7 1.3 fusion.227
  182.0 1.4 fusion.227
  184.4 1.4 fusion.227
  186.7 1.4 fusion.227
  189.1 1.4 fusion.227
  191.4 1.4 fusion.227
  193.8 1.4 fusion.227
  196.1 1.4 fusion.227
  198.5 1.4 fusion.156
  199.9 1.5 dynamic_update_slice.41
  201.3 1.5 dynamic_update_slice.40
  202.8 1.4 convert_element_type.50
  204.2 124.3 %pmax.7 = bf16[1,8,1024]{2,1,0:T(8,128)(2,1)} all-reduce(bf16[1,8,1024]{2,1,0:T(8,128)(2,1)} %convert_element_type.50), channel_id=1, replica_groups=mesh['seq'=32,'head'=8] {'seq'}, use_global_device_ids=true, to_apply=%region_20.21 | all-reduce | flops 8192 | bytes 32768 | tf_op jit(solution)/shard_map/pmax | solution.py:186
  328.5 1.4 fusion.147
  329.9 128.5 %psum.35 = f32[1,8,1024]{2,1,0:T(8,128)} all-reduce(f32[1,8,1024]{2,1,0:T(8,128)} %fusion.147), channel_id=1, replica_groups=mesh['seq'=32,'head'=8] {'seq'}, use_global_device_ids=true, to_apply=%region_22.23 | all-reduce | flops 8192 | bytes 65536 | tf_op jit(solution)/shard_map/psum | solution.py:187
  460.4 31.5 %while.77 = (s32[]{:T(128)}, f32[8,1,8,128]{3,2,1,0:T(8,128)}, bf16[8,128,1,8,128]{4,1,3,2,0:T(8,128)(2,1)}, bf16[256,1,128]{2,0,1:T(8,128)(2,1)S(1)}, f32[8,1,8...) while((s32[]{:T(128)}, f32[8,1,8,128]{3,2,1,0:T(8,128)}, ...), condition=%wide.region_25.26_spmd, body=%wide.region_23.25_spmd.sunk | while | flops 135265280 | bytes 2777197 | solution.py:192
  462.4 1.4 fusion.233
  466.3 1.4 fusion.233
  470.2 1.4 fusion.233
  474.2 1.4 fusion.233
  478.1 1.4 fusion.233
  482.0 1.4 fusion.233
  486.0 1.4 fusion.233
  489.9 1.4 fusion.233
  491.9 2.6 multiply_reduce_fusion
  494.5 1.4 bitcast_add_fusion.1
  495.8 1.5 dynamic_update_slice.42
  497.3 128.6 %psum.36 = f32[1,8,1024]{2,1,0:T(8,128)} all-reduce(f32[1,8,1024]{2,1,0:T(8,128)} %dynamic_update_slice.42), channel_id=1, replica_groups=mesh['seq'=32,'head'=8] {'seq'}, use_global_device_ids=true, to_apply=%region_27.28 | all-reduce | flops 8192 | bytes 65536 | tf_op jit(solution)/shard_map/psum | solution.py:203
  625.9 63.3 %while.79 = (s32[]{:T(128)}, f32[256,1,128]{0,2,1:T(8,128)}, f32[256,1,128]{0,2,1:T(8,128)}, f32[8,128,1,8,128]{4,3,1,0,2:T(8,128)}, bf16[8,128,1,8,128]{4,1,3,2...) while((s32[]{:T(128)}, f32[256,1,128]{0,2,1:T(8,128)}, ...), condition=%wide.region_29.30_spmd.clone, body=%wide.region_28.29_spmd.clone.sunk | while | flops 337412096 | bytes 9134296 | solution.py:214
  627.9 1.9 fusion.262
  635.8 1.9 fusion.262
  642.4 1.3 fusion.259
  643.7 1.9 fusion.262
  650.3 1.3 fusion.259
  651.6 1.9 fusion.262
  659.5 1.9 fusion.262
  667.5 1.9 fusion.262
  675.4 1.9 fusion.262
  683.3 1.9 fusion.262
  689.2 5.1 copy.140
  695.0 39.1 %while.78 = (s32[]{:T(128)}, f32[256,1,8,128]{0,3,2,1:T(8,128)}, f32[8,128,1,128]{3,1,2,0:T(8,128)}, f32[8,128,1,128]{3,1,2,0:T(8,128)}, bf16[8,128,1,128]{3,1,2...) while((s32[]{:T(128)}, f32[256,1,8,128]{0,3,2,1:T(8,128)}, ...), condition=%wide.region_14.15_spmd.clone, body=%wide.region_13.14_spmd.clone.sunk | while | flops 338182144 | bytes 17548512 | solution.py:154
  734.1 2.5 copy.79
  736.6 2.1 fusion.114
  738.7 1.4 convolution_multiply_fusion.8
  740.1 2.5 copy.56
  742.7 2.6 add_convert_fusion
  749.5 140.1 %all-reduce.5 = (bf16[1024,128]{1,0:T(8,128)(2,1)S(1)}, bf16[1024,128]{1,0:T(8,128)(2,1)}) all-reduce(f32[1024,128]{1,0:T(8,128)} %fusion.104, f32[1024,128]{1,0:T(8,128)} %fusion.105), channel_id=1, replica_groups=mesh['seq'=32,'head'=8] {'seq'}, use_global_device_ids=true, to_apply=%region_31.32 | all-reduce | flops 262144 | bytes 1572864 | tf_op jit(solution)/shard_map/psum | solution.py:227
  890.9 2.4 fusion.111
  894.5 85.3 %all-reduce.4.cloned.1.call-done = f32[1024,1024]{1,0:T(8,128)} async-done(((f32[1024,1024]{1,0:T(8,128)}), f32[1024,1024]{1,0:T(8,128)}) %all-reduce.4.cloned.1.call-update) | async-done | bytes 4194320 | tf_op jit(solution)/shard_map/psum | solution.py:227
  979.8 1.6 fusion.134
  (354 shorter events, 161.2 us)
Async XLA Ops:
  7.2 103.2 %all-gather.3.cloned.1.call-start = ((), (), s32[]{:S(2)}) async-start(), calls=%async_computation.1 | async-start | bytes 2162688 | tf_op jit(solution)/shard_map/all_gather | solution.py:92
  9.3 81.7 %all-to-all-start = ((bf16[32,32,128]{2,1,0:T(8,128)(2,1)}), bf16[32,32,128]{2,1,0:T(8,128)(2,1)}, u32[]{:S(2)}, u32[]{:S(2)}) async-start(bf16[32,32,128]{2,1,0:T(8,128)(2,1)} %stack.2), calls=%async_computation | async-start | bytes 524288 | tf_op jit(solution)/shard_map/all_to_all | solution.py:15
  22.1 152.2 %all-gather.5.cloned.1.call-start = ((), (), s32[]{:S(2)}) async-start(), calls=%async_computation.2 | async-start | bytes 2162688 | tf_op jit(solution)/shard_map/all_gather | solution.py:93
  22.9 956.9 %all-reduce.4.cloned.1.call-start = ((), (), s32[]{:S(2)}) async-start(), calls=%async_computation.3 | async-start | bytes 8388608 | tf_op jit(solution)/shard_map/psum | solution.py:227
  68.7 9.2 copy-start.2
  68.7 9.2 copy-start.13
  78.4 1.9 copy-start.21
  78.4 4.6 copy-start.8
  79.0 1.3 copy-start.22
  79.0 2.6 copy-start.15
  81.7 5.8 copy-start.4
  83.0 8.0 copy-start.23
  108.1 1.5 copy-start.18
  459.1 1.3 copy-start.17
  626.6 4.5 copy-start.5
  632.3 1.4 copy-start.6
  634.5 4.5 copy-start.5
  640.2 1.4 copy-start.6
  642.4 4.5 copy-start.5
  648.2 1.4 copy-start.6
  650.3 4.5 copy-start.5
  656.1 1.4 copy-start.6
  658.2 4.5 copy-start.5
  664.0 1.4 copy-start.6
  666.1 4.5 copy-start.5
  671.9 1.4 copy-start.6
  674.1 4.5 copy-start.5
  679.8 1.4 copy-start.6
  682.0 4.5 copy-start.5
  687.7 1.4 copy-start.6
  694.3 0.7 copy-start.19
  695.3 3.0 copy-start
  698.8 1.1 copy-start.1
  700.2 3.0 copy-start
  703.7 1.1 copy-start.1
  705.1 3.0 copy-start
  708.6 1.1 copy-start.1
  710.0 3.0 copy-start
  713.5 1.1 copy-start.1
  714.9 3.0 copy-start
  718.4 1.1 copy-start.1
  719.8 3.0 copy-start
  723.2 1.1 copy-start.1
  724.7 3.0 copy-start
  728.1 1.1 copy-start.1
  729.6 3.0 copy-start
  733.0 1.1 copy-start.1
  734.1 2.5 copy-start.20
  738.7 1.4 copy-start.11
  740.1 6.0 copy-start.24
  742.7 3.5 copy-start.3
  742.7 3.5 copy-start.12
  745.3 1.5 copy-start.16
  745.3 1.5 copy-start.26
  746.4 1.6 copy-start.14
  746.5 1.6 copy-start.25
  746.9 2.4 copy-start.7
  746.9 2.5 copy-start.10
  749.3 144.1 %copy-start.9 = (bf16[256,1024]{1,0:T(8,128)(2,1)S(1)}, bf16[256,1024]{1,0:T(8,128)(2,1)}, u32[]{:S(2)}) copy-start(bf16[256,1024]{1,0:T(8,128)(2,1)} %param.24) | copy-start | bytes 1572868
Sparse Core Ops, SparseCore 0:
  10.8 84.1 all-gather.2
  97.8 76.5 all-gather.4
  694.4 285.2 all-reduce.3
